TPU v7x, 32 devices: a whole 2x2x4 slice. The times are simulated.
32 devices in a mesh: gx: 2 (over y), gy: 4 (over z), gz: 4 (over x, core).
Axes of the slice: x: 2, y: 2, z: 4, core: 2. Of those that a mesh axis runs over, the one named last changes fastest.
Arguments:
- source_term: float32 [32, 8, 32, 512], P(None, 'gx', 'gy', 'gz'), may hold values from -16 to 16
- labels: int32 [8, 32, 512], P('gx', 'gy', 'gz'), may hold values from 0 to 5
- conductivity_table: float32 [6], replicated, may hold values from 0.05 to 1
- send_map: int32 [2, 4, 4, 256], P('gx', 'gy', 'gz'), may hold values from -1 to 4095, as said below
- owner_slots: int32 [4096], P(('gx', 'gy', 'gz')), may hold values from 0 to 255, as said below
- sensor_data: float32 [32, 128], replicated, may hold values from -6 to 6
Outputs:
- projections: float32 [3, 128, 4096], P(None, None, ('gx', 'gy', 'gz'))
- gram_blocks: float32 [6, 4096], P(None, ('gx', 'gy', 'gz'))
Inputs may be any that keep to these rules, and one draw needn't show every extreme that they name: `send_map`: entries q * 32 to q * 32 + 31 of row (sx, sy, iz) hold, in their first slots, the brick-local voxels (i * 8 + j) * 128 + k of the positions that this brick sends to owner q = ix * 4 + iy of the same iz, and -1 in the others; no voxel appears twice in a row; some brick fills all 32 slots of some owner. `owner_slots`: the 128 entries of owner d = (ix * 4 + iy) * 4 + iz name, each once, exactly the slots src * 32 + slot that the bricks src = sx * 4 + sy with the same iz fill for it.
All inputs are finite; a program needn't handle non-finite values.
Results may differ from a plain program's by a relative error of at most 0.00012.
Values sent between devices are 32-bit elements; how exact they have to be, the bound alone decides.
No kernel may reach another device: no remote copies, remote signals or barrier semaphores. Data moves between devices by JAX's collectives and lax.ppermute only.
A program may use at most 64 MiB of HBM per device.

v0:
```python
import jax
import jax.numpy as jnp
from jax import lax
from jax.sharding import PartitionSpec as P

mass_term = 0.25


def extended(block, sides, width):
    for axis, dim in sides:
        count = lax.axis_size(axis)
        forward = [(i, i + 1) for i in range(count - 1)]
        backward = [(target, source) for source, target in forward]
        low = lax.ppermute(
            lax.slice_in_dim(block, block.shape[dim] - width, None, axis=dim), axis, forward
        )
        high = lax.ppermute(lax.slice_in_dim(block, 0, width, axis=dim), axis, backward)
        block = jnp.concatenate([low, block, high], axis=dim)
    return block


def tissue(shifted, table):
    conductivity = jnp.zeros(shifted.shape, table.dtype)
    for tissue_level in range(table.shape[0]):
        conductivity = conductivity + jnp.where(
            shifted == tissue_level + 1, table[tissue_level], 0.0
        )
    inside = (shifted > 0).astype(table.dtype)
    return (conductivity, inside)


def neighbour_slices(dim_index, offset):
    selection = [slice(1, -1), slice(1, -1), slice(1, -1)]
    selection[dim_index] = slice(2, None) if offset > 0 else slice(0, -2)
    return tuple(selection)


def stencil(padded, conductivity, inside):
    leading = (slice(None),) * (padded.ndim - 3)
    middle = (slice(1, -1), slice(1, -1), slice(1, -1))
    centre = padded[leading + middle]
    own_cond = conductivity[middle]
    own_in = inside[middle]
    accumulated = mass_term * centre
    for dim_index in range(3):
        for offset in (-1, 1):
            beside_all = neighbour_slices(dim_index, offset)
            weight = 0.5 * (own_cond + conductivity[beside_all]) * own_in * inside[beside_all]
            accumulated = accumulated + weight * (centre - padded[leading + beside_all])
    return accumulated


def gram_rows(leadfield):
    entry_pairs = ((0, 0), (1, 1), (2, 2), (0, 1), (0, 2), (1, 2))
    return jnp.stack(
        [jnp.sum(leadfield[first] * leadfield[second], axis=0) for first, second in entry_pairs]
    )


def local_inner(first, second):
    return jnp.sum(first * second, axis=(1, 2, 3))


def per_sensor(values):
    return values[:, None, None, None]


def per_device(source_term, labels, conductivity_table, send_map, owner_slots, sensor_data):
    sensors, size_x, size_y, size_z = source_term.shape
    shifted = labels + 1
    label_pad = extended(shifted, (("gx", 0), ("gy", 1), ("gz", 2)), 2)
    conductivity, inside = tissue(label_pad, conductivity_table)
    source_pad = extended(source_term, (("gx", 1), ("gy", 2), ("gz", 3)), 2)
    applied = stencil(source_pad, conductivity, inside)
    inner_cond = conductivity[1:-1, 1:-1, 1:-1]
    inner_in = inside[1:-1, 1:-1, 1:-1]
    twice_applied = stencil(applied, inner_cond, inner_in)
    applied_core = applied[:, 1:-1, 1:-1, 1:-1]
    moment_zero, moment_one, moment_two, moment_three = lax.psum(
        (
            local_inner(source_term, source_term),
            local_inner(source_term, applied_core),
            local_inner(applied_core, applied_core),
            local_inner(applied_core, twice_applied),
        ),
        ("gx", "gy", "gz"),
    )
    first_step = moment_zero / moment_one
    residue = first_step * first_step * moment_two - moment_zero
    growth = 1.0 + residue / moment_zero
    curvature = (
        growth * growth * moment_one
        - 2.0 * growth * first_step * moment_two
        + first_step * first_step * moment_three
    )
    second_step = residue / curvature
    source_coef = first_step + second_step * growth
    applied_coef = second_step * first_step
    solution_pad = (
        per_sensor(source_coef) * source_pad[:, 1:-1, 1:-1, 1:-1]
        - per_sensor(applied_coef) * applied
    )
    cond_inner = conductivity[2:-2, 2:-2, 2:-2]
    voxel_local = jnp.maximum(send_map.reshape(-1), 0)
    index_x = voxel_local // (size_y * size_z)
    index_y = voxel_local // size_z % size_y
    index_z = voxel_local % size_z
    stride_y = size_z + 2
    stride_x = (size_y + 2) * (size_z + 2)
    centre = (index_x + 1) * stride_x + (index_y + 1) * stride_y + (index_z + 1)
    flattened = solution_pad.reshape(sensors, -1)
    cond_here = jnp.take(cond_inner.reshape(-1), voxel_local)

    def gradient(stride):
        upper = jnp.take(flattened, centre + stride, axis=1)
        lower = jnp.take(flattened, centre - stride, axis=1)
        return cond_here * ((upper - lower) * 0.5)

    columns = jnp.stack([gradient(stride_x), gradient(stride_y), gradient(1)])
    received = lax.all_to_all(columns, ("gx", "gy"), split_axis=2, concat_axis=2, tiled=True)
    owned = jnp.take(received, owner_slots, axis=2)
    projections = jnp.einsum("csp,st->ctp", owned, sensor_data, precision=lax.Precision.HIGHEST)
    return (projections, gram_rows(owned))


def solution(mesh):
    in_specs = (
        P(None, "gx", "gy", "gz"),
        P("gx", "gy", "gz"),
        P(),
        P("gx", "gy", "gz", None),
        P(("gx", "gy", "gz")),
        P(),
    )
    out_specs = (P(None, None, ("gx", "gy", "gz")), P(None, ("gx", "gy", "gz")))
    return jax.shard_map(
        per_device, mesh=mesh, in_specs=in_specs, out_specs=out_specs, check_vma=False
    )
```

profile of v0, /device:TPU:0, one launch (start us, length us, event | category | flops | bytes accessed | tf_op | source)
XLA Modules:
  0.0 188.7 jit_solution(1903327529436321746)
XLA Ops:
  1.4 4.9 %collective-permute-start.6 = (s32[2,8,128]{2,1,0:T(8,128)S(1)}, s32[2,8,128]{2,1,0:T(8,128)S(1)}, u32[]{:S(2)}, u32[]{:S(2)}) collective-permute-start(s32[2,8,128]{2,1,0:T(8,128)S(1)} %get-tuple-element.58), channel_id=1, source_target_pairs={{0,16},{1,17},{2,18},{3,19},{4,20},{5,21},{6,22},{7,23},{8,24},{9,... | collective-permute-start | bytes 24584 | tf_op jit(solution)/shard_map/ppermute | solution.py:14
  6.3 1.3 collective-permute-start.7
  7.6 1.1 fusion.70
  8.7 4.6 %collective-permute-start = (f32[32,2,8,128]{3,2,1,0:T(8,128)S(1)}, f32[32,2,8,128]{3,2,1,0:T(8,128)S(1)}, u32[]{:S(2)}, u32[]{:S(2)}) collective-permute-start(f32[32,2,8,128]{3,2,1,0:T(8,128)S(1)} %get-tuple-element.39), channel_id=1, source_target_pairs={{0,16},{1,17},{2,18},{3,19},{4,20},{5,21},{6,22},{7,23},{8,24},{9,... | collective-permute-start | bytes 786440 | tf_op jit(solution)/shard_map/ppermute | solution.py:14
  13.2 1.3 collective-permute-start.1
  14.5 1.9 multiply_reduce_fusion.2
  19.6 1.5 fusion.73
  23.0 3.5 %collective-permute-start.8 = (s32[8,2,128]{2,1,0:T(2,128)S(1)}, s32[8,2,128]{2,1,0:T(2,128)S(1)}, u32[]{:S(2)}, u32[]{:S(2)}) collective-permute-start(s32[8,2,128]{2,1,0:T(2,128)S(1)} %get-tuple-element.56), channel_id=1, source_target_pairs={{0,4},{4,8},{8,12},{1,5},{5,9},{9,13},{2,6},{6,10},{10,14},{3,7},{... | collective-permute-start | bytes 24584 | tf_op jit(solution)/shard_map/ppermute | solution.py:14
  26.4 1.3 collective-permute-start.9
  28.3 3.6 %collective-permute-done.9 = s32[8,2,128]{2,1,0:T(2,128)S(1)} collective-permute-done((s32[8,2,128]{2,1,0:T(2,128)S(1)}, s32[8,2,128]{2,1,0:T(2,128)S(1)}, u32[]{:S(2)}, u32[]{:S(2)}) %collective-permute-start.9) | collective-permute-done | bytes 8224 | tf_op jit(solution)/shard_map/ppermute | solution.py:17
  32.1 1.3 collective-permute-start.10
  33.4 1.3 collective-permute-start.11
  34.7 1.2 copy.105
  35.9 2.4 %collective-permute-done.11 = s32[8,12,2]{2,1,0:T(8,128)S(1)} collective-permute-done((s32[8,12,2]{2,1,0:T(8,128)S(1)}, s32[8,12,2]{2,1,0:T(8,128)S(1)}, u32[]{:S(2)}, u32[]{:S(2)}) %collective-permute-start.11) | collective-permute-done | bytes 800 | tf_op jit(solution)/shard_map/ppermute | solution.py:17
  38.4 3.8 %select_add_fusion = f32[8,12,132]{2,1,0:T(8,128)S(1)} fusion(f32[]{:T(128)} %bitcast.8, f32[]{:T(128)} %bitcast.7, f32[]{:T(128)} %bitcast.6, f32[]{:T(128)} %bitcast.5, f32[]{:T(128)} %bitcast.4, f32[]{:T(128)} %bitcast.3, s32[8,12,2]{2,1,0:T(8,128)S(1)} %collective-permute-done.11, s32[8,2,128]{2,1,0:T(2,128)S(1)} %collective-permute-done.9, ...), kind=kLoop, calls=%fused_computation.79 | loop fusion | flops 291456 | bytes 101400 | tf_op jit(solution)/shard_map/add | solution.py:25
  42.2 0.7 slice_multiply_fusion.11
  43.7 3.5 %collective-permute-start.2 = (f32[32,8,2,128]{3,1,2,0:T(8,128)S(1)}, f32[32,8,2,128]{3,1,2,0:T(8,128)S(1)}, u32[]{:S(2)}, u32[]{:S(2)}) collective-permute-start(f32[32,8,2,128]{3,1,2,0:T(8,128)S(1)} %get-tuple-element.37), channel_id=1, source_target_pairs={{0,4},{4,8},{8,12},{1,5},{5,9},{9,13},{2,6},{6,10},{10,14},{3,7},{... | collective-permute-start | bytes 786440 | tf_op jit(solution)/shard_map/ppermute | solution.py:14
  47.2 1.3 collective-permute-start.3
  49.2 1.7 gather_fusion
  51.9 4.7 %collective-permute-done.3 = f32[32,8,2,128]{3,1,2,0:T(8,128)S(1)} collective-permute-done((f32[32,8,2,128]{3,1,2,0:T(8,128)S(1)}, f32[32,8,2,128]{3,1,2,0:T(8,128)S(1)}, u32[]{:S(2)}, u32[]{:S(2)}) %collective-permute-start.3) | collective-permute-done | bytes 262176 | tf_op jit(solution)/shard_map/ppermute | solution.py:17
  57.6 1.8 fusion.69
  59.4 2.2 %copy.93 = f32[32,8,12,2]{0,1,3,2:T(8,128)S(1)} copy(f32[32,8,12,2]{3,1,2,0:T(8,128)} %get-tuple-element.35) | data formatting | bytes 49152 | tf_op jit(solution)/shard_map/slice | solution.py:15
  61.6 0.9 copy.94
  62.5 1.3 collective-permute-start.5
  63.8 4.2 %collective-permute-start.4 = (f32[32,8,12,2]{0,1,3,2:T(8,128)S(1)}, f32[32,8,12,2]{0,1,3,2:T(8,128)S(1)}, u32[]{:S(2)}, u32[]{:S(2)}) collective-permute-start(f32[32,8,12,2]{0,1,3,2:T(8,128)S(1)} %copy.93), channel_id=1, source_target_pairs={{0,1},{1,2},{2,3},{4,5},{5,6},{6,7},{8,9},{9,10},{10,11},{12,13},{... | collective-permute-start | bytes 73736 | tf_op jit(solution)/shard_map/ppermute | solution.py:14
  74.5 2.4 %copy.95 = f32[32,8,12,2]{3,1,2,0:T(8,128)} copy(f32[32,8,12,2]{0,1,3,2:T(8,128)S(1)} %collective-permute-done.4) | data formatting | bytes 49152 | tf_op jit(solution)/shard_map/ppermute | solution.py:14
  76.8 2.4 %copy.96 = f32[32,8,12,2]{3,1,2,0:T(8,128)} copy(f32[32,8,12,2]{0,1,3,2:T(8,128)S(1)} %collective-permute-done.5) | data formatting | bytes 49152 | tf_op jit(solution)/shard_map/ppermute | solution.py:17
  79.3 4.8 %pad_maximum_fusion = f32[32,8,12,132]{3,1,2,0:T(8,128)S(1)} fusion(f32[32,8,12,2]{3,1,2,0:T(8,128)} %copy.96, f32[32,8,2,128]{3,1,2,0:T(8,128)} %copy-done.11, f32[32,2,8,128]{3,1,2,0:T(2,128)} %copy-done.7, f32[32,4,8,128]{3,1,2,0:T(4,128)} %copy-done.4, f32[32,2,8,128]{3,1,2,0:T(2,128)S(1)} %copy.90, f32[32,8,2,128]{3,1,2,0:T(8,128)} %copy-done.9, ...), kind=kLoop, calls=%fused_computation.8 | loop fusion | flops 2433024 | bytes 3244032 | tf_op jit(solution)/shard_map/concatenate | solution.py:18
  84.3 7.2 %fusion.2 = f32[32,6,10,130]{3,1,2,0:T(8,128)S(1)} fusion(f32[32,8,12,2]{3,1,2,0:T(8,128)S(1)} %copy-done.3, f32[32,8,2,128]{3,1,2,0:T(8,128)S(1)} %copy-done.12, f32[32,8,2,128]{3,1,2,0:T(8,128)S(1)} %copy-done.10, f32[32,2,8,128]{3,1,2,0:T(2,128)S(1)} %copy-done.8, f32[32,4,8,128]{3,1,2,0:T(4,128)S(1)} %copy-done.5, f32[32,2,8,128]{3,1,2,0:T(2,128)S(1)} %copy.90, ...), kind=kLoop, calls=%fused_computation.12 | loop fusion | flops 7238400 | bytes 7799616 | tf_op jit(solution)/shard_map/add | solution.py:49
  91.5 1.5 copy-done.1
  93.1 2.4 %multiply_reduce_fusion.1 = (f32[32]{0:T(128)S(1)}, f32[32]{0:T(128)S(1)}, f32[32]{0:T(128)S(1)}) fusion(f32[32,6,10,130]{3,1,2,0:T(8,128)S(1)} %fusion.2, f32[32,4,8,128]{3,2,1,0:T(8,128)S(1)} %copy-done.6, f32[4,8,128]{2,0,1:T(4,128)S(1)} %copy.111, f32[4,8,128]{2,0,1:T(4,128)S(1)} %copy.110, f32[4,8,128]{2,0,1:T(4,128)S(1)} %copy-done.19, ...), kind=kLoop, calls=%fused_computation.60 | loop fusion | flops 3276704 | bytes 4292992 | tf_op jit(solution)/shard_map/reduce_sum | solution.py:61
  95.4 41.9 %all-reduce = (f32[32]{0:T(128)S(1)}, f32[32]{0:T(128)S(1)}, f32[32]{0:T(128)S(1)}, f32[32]{0:T(128)S(1)}) all-reduce(f32[32]{0:T(128)S(1)} %get-tuple-element.15, f32[32]{0:T(128)S(1)} %get-tuple-element.14, f32[32]{0:T(128)S(1)} %copy-done.32, f32[32]{0:T(128)S(1)} %get-tuple-element.13), channel_id=1, replica_groups=mesh['gx'=2,'gy'=4,'gz'=4] {'gx','gy','gz'}, use_global_device_ids=true, to_apply=%region_7.8 | all-reduce | flops 128 | bytes 1024 | tf_op jit(solution)/shard_map/psum | solution.py:79
  137.4 4.1 %multiply_subtract_fusion = f32[32,6,10,130]{3,1,2,0:T(8,128)} fusion(f32[32,6,10,130]{3,1,2,0:T(8,128)} %copy-done.1, f32[32,8,12,132]{3,1,2,0:T(8,128)S(1)} %pad_maximum_fusion, f32[32]{0:T(128)S(1)} %mul.415, f32[32]{0:T(128)S(1)} %get-tuple-element.31), kind=kLoop, calls=%fused_computation.37 | loop fusion | flops 748800 | bytes 2995456 | tf_op jit(solution)/shard_map/sub | solution.py:100
  141.5 4.8 %copy.122 = f32[32,6,10,130]{0,3,2,1:T(8,128)} copy(f32[32,6,10,130]{3,1,2,0:T(8,128)} %multiply_subtract_fusion) | data formatting | bytes 1996800 | tf_op jit(solution)/shard_map/reshape | solution.py:111
  146.3 4.8 %reshape.172 = f32[32,7800]{0,1:T(8,128)} reshape(f32[32,6,10,130]{0,3,2,1:T(8,128)} %copy.122) | data formatting | bytes 1996800 | tf_op jit(solution)/shard_map/reshape | solution.py:111
  151.1 3.0 %gather_fusion.7 = f32[256,32]{1,0:T(8,128)S(1)} fusion(f32[32,7800]{0,1:T(8,128)} %reshape.172, s32[1024]{0:T(1024)} %get-tuple-element.84), kind=kCustom, calls=%fused_computation.5.clone | custom fusion | bytes 66560 | tf_op jit(solution)/shard_map/jit(_take)/gather | solution.py:116
  154.1 3.0 %gather_fusion.6 = f32[256,32]{1,0:T(8,128)S(1)} fusion(f32[32,7800]{0,1:T(8,128)} %reshape.172, s32[1024]{0:T(1024)} %get-tuple-element.85), kind=kCustom, calls=%fused_computation.4.clone | custom fusion | bytes 66560 | tf_op jit(solution)/shard_map/jit(_take)/gather | solution.py:115
  157.1 3.0 %gather_fusion.5 = f32[256,32]{1,0:T(8,128)S(1)} fusion(f32[32,7800]{0,1:T(8,128)} %reshape.172, s32[1024]{0:T(1024)} %get-tuple-element.86), kind=kCustom, calls=%fused_computation.3.clone | custom fusion | bytes 66560 | tf_op jit(solution)/shard_map/jit(_take)/gather | solution.py:116
  160.1 3.0 %gather_fusion.4 = f32[256,32]{1,0:T(8,128)S(1)} fusion(f32[32,7800]{0,1:T(8,128)} %reshape.172, s32[1024]{0:T(1024)} %get-tuple-element.87), kind=kCustom, calls=%fused_computation.2.clone | custom fusion | bytes 66560 | tf_op jit(solution)/shard_map/jit(_take)/gather | solution.py:115
  163.1 3.0 %gather_fusion.3 = f32[256,32]{1,0:T(8,128)S(1)} fusion(f32[32,7800]{0,1:T(8,128)} %reshape.172, s32[1024]{0:T(1024)} %get-tuple-element.88), kind=kCustom, calls=%fused_computation.1.clone | custom fusion | bytes 66560 | tf_op jit(solution)/shard_map/jit(_take)/gather | solution.py:116
  166.1 3.0 %gather_fusion.2 = f32[256,32]{1,0:T(8,128)S(1)} fusion(f32[32,7800]{0,1:T(8,128)} %reshape.172, s32[1024]{0:T(1024)} %get-tuple-element.89), kind=kCustom, calls=%fused_computation.clone | custom fusion | bytes 66560 | tf_op jit(solution)/shard_map/jit(_take)/gather | solution.py:115
  169.8 1.0 reshape.176
  170.8 4.5 %all-to-all-start = ((f32[8,1,3072]{2,1,0:T(1,128)}), f32[8,1,3072]{2,1,0:T(1,128)S(1)}, u32[]{:S(2)}, u32[]{:S(2)}) async-start(f32[8,1,3072]{2,1,0:T(1,128)} %reshape.176), calls=%async_computation | async-start | bytes 196608 | tf_op jit(solution)/shard_map/all_to_all | solution.py:120
  175.3 7.2 %all-to-all-done = f32[8,1,3072]{2,1,0:T(1,128)S(1)} async-done(((f32[8,1,3072]{2,1,0:T(1,128)}), f32[8,1,3072]{2,1,0:T(1,128)S(1)}, u32[]{:S(2)}, u32[]{:S(2)}) %all-to-all-start) | async-done | bytes 98336 | tf_op jit(solution)/shard_map/all_to_all | solution.py:120
  183.0 0.9 reduce.12
  184.3 0.9 gather_fusion.1
  185.3 1.6 multiply_reduce_fusion.3
  187.3 0.8 copy.121
  (127 shorter events, 19.2 us)
Async XLA Ops:
  0.6 186.3 %copy-start = (f32[32,128]{1,0:T(8,128)S(1)}, f32[32,128]{1,0:T(8,128)}, u32[]{:S(2)}) copy-start(f32[32,128]{1,0:T(8,128)} %param.13) | copy-start | bytes 49156
  1.4 21.6 %collective-permute-start.6 = (s32[2,8,128]{2,1,0:T(8,128)S(1)}, s32[2,8,128]{2,1,0:T(8,128)S(1)}, u32[]{:S(2)}, u32[]{:S(2)}) collective-permute-start(s32[2,8,128]{2,1,0:T(8,128)S(1)} %get-tuple-element.58), channel_id=1, source_target_pairs={{0,16},{1,17},{2,18},{3,19},{4,20},{5,21},{6,22},{7,23},{8,24},{9,... | collective-permute-start | bytes 24584 | tf_op jit(solution)/shard_map/ppermute | solution.py:14
  6.3 16.7 %collective-permute-start.7 = (s32[2,8,128]{2,1,0:T(8,128)S(1)}, s32[2,8,128]{2,1,0:T(8,128)S(1)}, u32[]{:S(2)}, u32[]{:S(2)}) collective-permute-start(s32[2,8,128]{2,1,0:T(8,128)S(1)} %get-tuple-element.59), channel_id=1, source_target_pairs={{16,0},{17,1},{18,2},{19,3},{20,4},{21,5},{22,6},{23,7},{24,8},{25... | collective-permute-start | bytes 24584 | tf_op jit(solution)/shard_map/ppermute | solution.py:17
  8.7 34.5 %collective-permute-start = (f32[32,2,8,128]{3,2,1,0:T(8,128)S(1)}, f32[32,2,8,128]{3,2,1,0:T(8,128)S(1)}, u32[]{:S(2)}, u32[]{:S(2)}) collective-permute-start(f32[32,2,8,128]{3,2,1,0:T(8,128)S(1)} %get-tuple-element.39), channel_id=1, source_target_pairs={{0,16},{1,17},{2,18},{3,19},{4,20},{5,21},{6,22},{7,23},{8,24},{9,... | collective-permute-start | bytes 786440 | tf_op jit(solution)/shard_map/ppermute | solution.py:14
  13.2 30.1 %collective-permute-start.1 = (f32[32,2,8,128]{3,2,1,0:T(8,128)S(1)}, f32[32,2,8,128]{3,2,1,0:T(8,128)S(1)}, u32[]{:S(2)}, u32[]{:S(2)}) collective-permute-start(f32[32,2,8,128]{3,2,1,0:T(8,128)S(1)} %get-tuple-element.40), channel_id=1, source_target_pairs={{16,0},{17,1},{18,2},{19,3},{20,4},{21,5},{22,6},{23,7},{24,8},{25... | collective-permute-start | bytes 786440 | tf_op jit(solution)/shard_map/ppermute | solution.py:17
  23.0 5.4 %collective-permute-start.8 = (s32[8,2,128]{2,1,0:T(2,128)S(1)}, s32[8,2,128]{2,1,0:T(2,128)S(1)}, u32[]{:S(2)}, u32[]{:S(2)}) collective-permute-start(s32[8,2,128]{2,1,0:T(2,128)S(1)} %get-tuple-element.56), channel_id=1, source_target_pairs={{0,4},{4,8},{8,12},{1,5},{5,9},{9,13},{2,6},{6,10},{10,14},{3,7},{... | collective-permute-start | bytes 24584 | tf_op jit(solution)/shard_map/ppermute | solution.py:14
  26.4 5.5 %collective-permute-start.9 = (s32[8,2,128]{2,1,0:T(2,128)S(1)}, s32[8,2,128]{2,1,0:T(2,128)S(1)}, u32[]{:S(2)}, u32[]{:S(2)}) collective-permute-start(s32[8,2,128]{2,1,0:T(2,128)S(1)} %get-tuple-element.57), channel_id=1, source_target_pairs={{4,0},{8,4},{12,8},{5,1},{9,5},{13,9},{6,2},{10,6},{14,10},{7,3},{... | collective-permute-start | bytes 24584 | tf_op jit(solution)/shard_map/ppermute | solution.py:17
  32.1 3.8 %collective-permute-start.10 = (s32[8,12,2]{2,1,0:T(8,128)S(1)}, s32[8,12,2]{2,1,0:T(8,128)S(1)}, u32[]{:S(2)}, u32[]{:S(2)}) collective-permute-start(s32[8,12,2]{2,1,0:T(8,128)S(1)} %get-tuple-element.54), channel_id=1, source_target_pairs={{0,1},{1,2},{2,3},{4,5},{5,6},{6,7},{8,9},{9,10},{10,11},{12,13},{... | collective-permute-start | bytes 2312 | tf_op jit(solution)/shard_map/ppermute | solution.py:14
  33.4 4.9 %collective-permute-start.11 = (s32[8,12,2]{2,1,0:T(8,128)S(1)}, s32[8,12,2]{2,1,0:T(8,128)S(1)}, u32[]{:S(2)}, u32[]{:S(2)}) collective-permute-start(s32[8,12,2]{2,1,0:T(8,128)S(1)} %get-tuple-element.55), channel_id=1, source_target_pairs={{1,0},{2,1},{3,2},{5,4},{6,5},{7,6},{9,8},{10,9},{11,10},{13,12},{... | collective-permute-start | bytes 2312 | tf_op jit(solution)/shard_map/ppermute | solution.py:17
  35.9 20.7 %copy-start.4 = (f32[32,4,8,128]{3,1,2,0:T(4,128)}, f32[32,4,8,128]{3,1,2,0:T(4,128)S(1)}, u32[]{:S(2)}) copy-start(f32[32,4,8,128]{3,1,2,0:T(4,128)S(1)} %copy.105) | copy-start | bytes 1572868
  43.5 14.2 %copy-start.7 = (f32[32,2,8,128]{3,1,2,0:T(2,128)}, f32[32,2,8,128]{3,1,2,0:T(2,128)S(1)}, u32[]{:S(2)}) copy-start(f32[32,2,8,128]{3,1,2,0:T(2,128)S(1)} %copy.92) | copy-start | bytes 786436
  43.7 8.2 %collective-permute-start.2 = (f32[32,8,2,128]{3,1,2,0:T(8,128)S(1)}, f32[32,8,2,128]{3,1,2,0:T(8,128)S(1)}, u32[]{:S(2)}, u32[]{:S(2)}) collective-permute-start(f32[32,8,2,128]{3,1,2,0:T(8,128)S(1)} %get-tuple-element.37), channel_id=1, source_target_pairs={{0,4},{4,8},{8,12},{1,5},{5,9},{9,13},{2,6},{6,10},{10,14},{3,7},{... | collective-permute-start | bytes 786440 | tf_op jit(solution)/shard_map/ppermute | solution.py:14
  47.2 9.4 %collective-permute-start.3 = (f32[32,8,2,128]{3,1,2,0:T(8,128)S(1)}, f32[32,8,2,128]{3,1,2,0:T(8,128)S(1)}, u32[]{:S(2)}, u32[]{:S(2)}) collective-permute-start(f32[32,8,2,128]{3,1,2,0:T(8,128)S(1)} %get-tuple-element.38), channel_id=1, source_target_pairs={{4,0},{8,4},{12,8},{5,1},{9,5},{13,9},{6,2},{10,6},{14,10},{7,3},{... | collective-permute-start | bytes 786440 | tf_op jit(solution)/shard_map/ppermute | solution.py:17
  51.9 4.7 %copy-start.9 = (f32[32,8,2,128]{3,1,2,0:T(8,128)}, f32[32,8,2,128]{3,1,2,0:T(8,128)S(1)}, u32[]{:S(2)}) copy-start(f32[32,8,2,128]{3,1,2,0:T(8,128)S(1)} %collective-permute-done.2) | copy-start | bytes 786436
  56.6 0.7 copy-start.11
  59.4 9.2 %copy-start.25 = (f32[4,8,128]{2,1,0:T(8,128)S(1)}, f32[4,8,128]{2,1,0:T(8,128)}, u32[]{:S(2)}) copy-start(f32[4,8,128]{2,1,0:T(8,128)} %get-tuple-element.46) | copy-start | bytes 49156
  59.4 9.2 %copy-start.24 = (f32[4,8,128]{2,1,0:T(8,128)S(1)}, f32[4,8,128]{2,1,0:T(8,128)}, u32[]{:S(2)}) copy-start(f32[4,8,128]{2,1,0:T(8,128)} %get-tuple-element.41) | copy-start | bytes 49156
  59.4 9.8 %copy-start.23 = (f32[4,8,128]{2,1,0:T(8,128)S(1)}, f32[4,8,128]{2,1,0:T(8,128)}, u32[]{:S(2)}) copy-start(f32[4,8,128]{2,1,0:T(8,128)} %get-tuple-element.42) | copy-start | bytes 49156
  59.4 10.4 %copy-start.22 = (f32[4,8,128]{2,1,0:T(8,128)S(1)}, f32[4,8,128]{2,1,0:T(8,128)}, u32[]{:S(2)}) copy-start(f32[4,8,128]{2,1,0:T(8,128)} %get-tuple-element.43) | copy-start | bytes 49156
  62.5 14.3 %collective-permute-start.5 = (f32[32,8,12,2]{0,1,3,2:T(8,128)S(1)}, f32[32,8,12,2]{0,1,3,2:T(8,128)S(1)}, u32[]{:S(2)}, u32[]{:S(2)}) collective-permute-start(f32[32,8,12,2]{0,1,3,2:T(8,128)S(1)} %copy.94), channel_id=1, source_target_pairs={{1,0},{2,1},{3,2},{5,4},{6,5},{7,6},{9,8},{10,9},{11,10},{13,12},{... | collective-permute-start | bytes 73736 | tf_op jit(solution)/shard_map/ppermute | solution.py:17
  63.8 10.7 %collective-permute-start.4 = (f32[32,8,12,2]{0,1,3,2:T(8,128)S(1)}, f32[32,8,12,2]{0,1,3,2:T(8,128)S(1)}, u32[]{:S(2)}, u32[]{:S(2)}) collective-permute-start(f32[32,8,12,2]{0,1,3,2:T(8,128)S(1)} %copy.93), channel_id=1, source_target_pairs={{0,1},{1,2},{2,3},{4,5},{5,6},{6,7},{8,9},{9,10},{10,11},{12,13},{... | collective-permute-start | bytes 73736 | tf_op jit(solution)/shard_map/ppermute | solution.py:14
  79.2 4.9 %copy-start.2 = (f32[32,8,12,2]{3,1,2,0:T(8,128)S(1)}, f32[32,8,12,2]{3,1,2,0:T(8,128)}, u32[]{:S(2)}) copy-start(f32[32,8,12,2]{3,1,2,0:T(8,128)} %copy.95) | copy-start | bytes 73732
  79.2 4.9 %copy-start.3 = (f32[32,8,12,2]{3,1,2,0:T(8,128)S(1)}, f32[32,8,12,2]{3,1,2,0:T(8,128)}, u32[]{:S(2)}) copy-start(f32[32,8,12,2]{3,1,2,0:T(8,128)} %copy.96) | copy-start | bytes 73732
  79.2 4.9 %copy-start.5 = (f32[32,4,8,128]{3,1,2,0:T(4,128)S(1)}, f32[32,4,8,128]{3,1,2,0:T(4,128)}, u32[]{:S(2)}) copy-start(f32[32,4,8,128]{3,1,2,0:T(4,128)} %copy-done.4) | copy-start | bytes 1572868
  79.2 4.9 %copy-start.8 = (f32[32,2,8,128]{3,1,2,0:T(2,128)S(1)}, f32[32,2,8,128]{3,1,2,0:T(2,128)}, u32[]{:S(2)}) copy-start(f32[32,2,8,128]{3,1,2,0:T(2,128)} %copy-done.7) | copy-start | bytes 786436
  79.2 4.9 %copy-start.10 = (f32[32,8,2,128]{3,1,2,0:T(8,128)S(1)}, f32[32,8,2,128]{3,1,2,0:T(8,128)}, u32[]{:S(2)}) copy-start(f32[32,8,2,128]{3,1,2,0:T(8,128)} %copy-done.9) | copy-start | bytes 786436
  79.2 4.9 %copy-start.12 = (f32[32,8,2,128]{3,1,2,0:T(8,128)S(1)}, f32[32,8,2,128]{3,1,2,0:T(8,128)}, u32[]{:S(2)}) copy-start(f32[32,8,2,128]{3,1,2,0:T(8,128)} %copy-done.11) | copy-start | bytes 786436
  79.3 4.9 %copy-start.13 = (f32[6,10,130]{2,0,1:T(8,128)S(1)}, f32[6,10,130]{2,0,1:T(8,128)}, u32[]{:S(2)}) copy-start(f32[6,10,130]{2,0,1:T(8,128)} %copy.98) | copy-start | bytes 93604
  79.3 4.9 %copy-start.14 = (f32[6,10,130]{2,0,1:T(8,128)S(1)}, f32[6,10,130]{2,0,1:T(8,128)}, u32[]{:S(2)}) copy-start(f32[6,10,130]{2,0,1:T(8,128)} %copy.99) | copy-start | bytes 93604
  79.3 4.9 %copy-start.15 = (f32[6,10,130]{2,0,1:T(8,128)S(1)}, f32[6,10,130]{2,0,1:T(8,128)}, u32[]{:S(2)}) copy-start(f32[6,10,130]{2,0,1:T(8,128)} %copy.97) | copy-start | bytes 93604
  79.3 4.9 %copy-start.16 = (f32[6,10,130]{2,0,1:T(8,128)S(1)}, f32[6,10,130]{2,0,1:T(8,128)}, u32[]{:S(2)}) copy-start(f32[6,10,130]{2,0,1:T(8,128)} %copy.101) | copy-start | bytes 93604
  79.3 4.9 %copy-start.17 = (f32[6,10,130]{2,0,1:T(8,128)S(1)}, f32[6,10,130]{2,0,1:T(8,128)}, u32[]{:S(2)}) copy-start(f32[6,10,130]{2,0,1:T(8,128)} %copy.100) | copy-start | bytes 93604
  84.2 8.8 %copy-start.6 = (f32[32,4,8,128]{3,2,1,0:T(8,128)S(1)}, f32[32,4,8,128]{3,2,1,0:T(8,128)}, u32[]{:S(2)}) copy-start(f32[32,4,8,128]{3,2,1,0:T(8,128)} %param.8) | copy-start | bytes 1572868
  84.2 8.8 %copy-start.18 = (f32[4,8,128]{2,0,1:T(4,128)S(1)}, f32[4,8,128]{2,0,1:T(4,128)}, u32[]{:S(2)}) copy-start(f32[4,8,128]{2,0,1:T(4,128)} %copy.106) | copy-start | bytes 49156
  84.2 8.8 %copy-start.19 = (f32[4,8,128]{2,0,1:T(4,128)S(1)}, f32[4,8,128]{2,0,1:T(4,128)}, u32[]{:S(2)}) copy-start(f32[4,8,128]{2,0,1:T(4,128)} %copy.109) | copy-start | bytes 49156
  84.2 8.8 %copy-start.20 = (f32[4,8,128]{2,0,1:T(4,128)S(1)}, f32[4,8,128]{2,0,1:T(4,128)}, u32[]{:S(2)}) copy-start(f32[4,8,128]{2,0,1:T(4,128)} %copy.108) | copy-start | bytes 49156
  84.3 8.8 %copy-start.21 = (f32[4,8,128]{2,0,1:T(4,128)S(1)}, f32[4,8,128]{2,0,1:T(4,128)}, u32[]{:S(2)}) copy-start(f32[4,8,128]{2,0,1:T(4,128)} %copy.107) | copy-start | bytes 49156
  91.5 1.5 copy-start.1
  93.0 2.4 %copy-start.32 = (f32[32]{0:T(128)S(1)}, f32[32]{0:T(128)}, u32[]{:S(2)}) copy-start(f32[32]{0:T(128)} %multiply_reduce_fusion.2) | copy-start | bytes 388
  146.3 22.8 %copy-start.26 = (f32[256]{0:T(256)S(1)}, f32[256]{0:T(256)}, u32[]{:S(2)}) copy-start(f32[256]{0:T(256)} %select_multiply_fusion) | copy-start | bytes 3076
  146.3 22.8 %copy-start.27 = (pred[256]{0:T(512)(128)(4,1)S(1)}, pred[256]{0:T(512)(128)(4,1)}, u32[]{:S(2)}) copy-start(pred[256]{0:T(512)(128)(4,1)} %get-tuple-element.63) | copy-start | bytes 772
  146.3 22.8 %copy-start.28 = (pred[256]{0:T(512)(128)(4,1)S(1)}, pred[256]{0:T(512)(128)(4,1)}, u32[]{:S(2)}) copy-start(pred[256]{0:T(512)(128)(4,1)} %get-tuple-element.64) | copy-start | bytes 772
  146.3 22.8 %copy-start.29 = (pred[256]{0:T(512)(128)(4,1)S(1)}, pred[256]{0:T(512)(128)(4,1)}, u32[]{:S(2)}) copy-start(pred[256]{0:T(512)(128)(4,1)} %get-tuple-element.65) | copy-start | bytes 772
  146.3 22.8 %copy-start.30 = (pred[256]{0:T(512)(128)(4,1)S(1)}, pred[256]{0:T(512)(128)(4,1)}, u32[]{:S(2)}) copy-start(pred[256]{0:T(512)(128)(4,1)} %get-tuple-element.66) | copy-start | bytes 772
  146.3 22.8 %copy-start.31 = (pred[256]{0:T(512)(128)(4,1)S(1)}, pred[256]{0:T(512)(128)(4,1)}, u32[]{:S(2)}) copy-start(pred[256]{0:T(512)(128)(4,1)} %get-tuple-element.67) | copy-start | bytes 772
  146.3 22.8 %copy-start.33 = (pred[256]{0:T(512)(128)(4,1)S(1)}, pred[256]{0:T(512)(128)(4,1)}, u32[]{:S(2)}) copy-start(pred[256]{0:T(512)(128)(4,1)} %get-tuple-element.29) | copy-start | bytes 772
  154.1 21.2 %copy-start.34 = (s32[128]{0:T(128)S(1)}, s32[128]{0:T(128)}, u32[]{:S(2)}) copy-start(s32[128]{0:T(128)} %param.12) | copy-start | bytes 1540
  170.8 11.8 %all-to-all-start = ((f32[8,1,3072]{2,1,0:T(1,128)}), f32[8,1,3072]{2,1,0:T(1,128)S(1)}, u32[]{:S(2)}, u32[]{:S(2)}) async-start(f32[8,1,3072]{2,1,0:T(1,128)} %reshape.176), calls=%async_computation | async-start | bytes 196608 | tf_op jit(solution)/shard_map/all_to_all | solution.py:120
where the time goes:
time: 190 us; the launch traced here: 189 us
  local copies, waits for them, and re-layouts  55.5 us (29%)
  blocking collectives  41.9 us (22%)
  other arithmetic  36.8 us (19%)
  starting transfers between devices  34.2 us (18%)
  waiting for transfers between devices  18.6 us (10%)
    psum x1, blocking collectives, per_device(): lax.psum((local_inner(source_term, source_term), local_inner(source_term,...  41.9 us
    ppermute x6, starting transfers between devices, extended(): lax.ppermute(lax.slice_in_dim(block, block.shape[dim] - width, None, axis...  21.9 us
    ppermute x6, waiting for transfers between devices, extended(): lax.ppermute(lax.slice_in_dim(block, 0, width, axis=dim), axis, backward)  10.7 us
    reshape x2, local copies, waits for them, and re-layouts, per_device(): flattened = solution_pad.reshape(sensors, -1)  9.57 us
    gather x3, local copies, waits for them, and re-layouts, gradient(): upper = jnp.take(flattened, centre + stride, axis=1)  8.98 us
    gather x3, local copies, waits for them, and re-layouts, gradient(): lower = jnp.take(flattened, centre - stride, axis=1)  8.97 us
    ppermute x6, starting transfers between devices, extended(): lax.ppermute(lax.slice_in_dim(block, 0, width, axis=dim), axis, backward)  7.75 us
    all_to_all x1, waiting for transfers between devices, per_device(): lax.all_to_all(columns, ('gx', 'gy'), split_axis=2, concat_axis=2, tiled=...  7.24 us
  transfers between devices with their start and end apart: 13, of which 5 were waited for; matrix products, arithmetic and copies ran while one was open for 15% of the time, Pallas kernels for 0%

commit v1 on v0

--- a/solution.py
+++ b/solution.py
@@ -1,9 +1,19 @@
+import functools
 import jax
 import jax.numpy as jnp
 from jax import lax
 from jax.sharding import PartitionSpec as P
 
 mass_term = 0.25
+
+
+def cycles_answer(view, mesh_ax, mesh_name):
+    for no in (mesh_ax, mesh_name):
+        view = lax.psum(view, no)
+    return view
+
+
+arrange_floor = functools.partial(cycles_answer, mesh_ax=("gy", "gz"), mesh_name="gx")
 
 
 def extended(block, sides, width):
@@ -76,14 +86,13 @@
     inner_in = inside[1:-1, 1:-1, 1:-1]
     twice_applied = stencil(applied, inner_cond, inner_in)
     applied_core = applied[:, 1:-1, 1:-1, 1:-1]
-    moment_zero, moment_one, moment_two, moment_three = lax.psum(
+    moment_zero, moment_one, moment_two, moment_three = arrange_floor(
         (
             local_inner(source_term, source_term),
             local_inner(source_term, applied_core),
             local_inner(applied_core, applied_core),
             local_inner(applied_core, twice_applied),
-        ),
-        ("gx", "gy", "gz"),
+        )
     )
     first_step = moment_zero / moment_one
     residue = first_step * first_step * moment_two - moment_zero

time: 190 us -> 184 us (0.968)
  blocking collectives: 41.9 us -> 37 us
    psum x1 -> x2, blocking collectives: 41.9 us -> 37 us  [cycles_answer(): view = lax.psum(view, no)]
where the time goes in v1:
time: 184 us; the launch traced here: 183 us
  local copies, waits for them, and re-layouts  55.5 us (30%)
  other arithmetic  37 us (20%)
  blocking collectives  37 us (20%)
  starting transfers between devices  33 us (18%)
  waiting for transfers between devices  18.6 us (10%)
    psum x2, blocking collectives, cycles_answer(): view = lax.psum(view, no)  37 us
    ppermute x6, starting transfers between devices, extended(): lax.ppermute(lax.slice_in_dim(block, block.shape[dim] - width, None, axis...  21.9 us
    ppermute x6, waiting for transfers between devices, extended(): lax.ppermute(lax.slice_in_dim(block, 0, width, axis=dim), axis, backward)  10.7 us
    reshape x2, local copies, waits for them, and re-layouts, per_device(): flattened = solution_pad.reshape(sensors, -1)  9.56 us
    gather x3, local copies, waits for them, and re-layouts, gradient(): upper = jnp.take(flattened, centre + stride, axis=1)  8.98 us
    gather x3, local copies, waits for them, and re-layouts, gradient(): lower = jnp.take(flattened, centre - stride, axis=1)  8.97 us
    ppermute x6, starting transfers between devices, extended(): lax.ppermute(lax.slice_in_dim(block, 0, width, axis=dim), axis, backward)  7.75 us
    add x1, other arithmetic, stencil(): accumulated = accumulated + weight * (centre - padded[leading + beside_all])  7.22 us
  transfers between devices with their start and end apart: 13, of which 5 were waited for; matrix products, arithmetic and copies ran while one was open for 15% of the time, Pallas kernels for 0%

profile of v1, /device:TPU:0, one launch (start us, length us, event | category | flops | bytes accessed | tf_op | source)
XLA Modules:
  0.0 182.8 jit_solution(5269733238857885998)
XLA Ops:
  1.4 4.9 %collective-permute-start.6 = (s32[2,8,128]{2,1,0:T(8,128)S(1)}, s32[2,8,128]{2,1,0:T(8,128)S(1)}, u32[]{:S(2)}, u32[]{:S(2)}) collective-permute-start(s32[2,8,128]{2,1,0:T(8,128)S(1)} %get-tuple-element.62), channel_id=1, source_target_pairs={{0,16},{1,17},{2,18},{3,19},{4,20},{5,21},{6,22},{7,23},{8,24},{9,... | collective-permute-start | bytes 24584 | tf_op jit(solution)/shard_map/ppermute | solution.py:24
  6.3 1.3 collective-permute-start.7
  7.6 1.1 fusion.70
  8.7 4.6 %collective-permute-start = (f32[32,2,8,128]{3,2,1,0:T(8,128)S(1)}, f32[32,2,8,128]{3,2,1,0:T(8,128)S(1)}, u32[]{:S(2)}, u32[]{:S(2)}) collective-permute-start(f32[32,2,8,128]{3,2,1,0:T(8,128)S(1)} %get-tuple-element.43), channel_id=1, source_target_pairs={{0,16},{1,17},{2,18},{3,19},{4,20},{5,21},{6,22},{7,23},{8,24},{9,... | collective-permute-start | bytes 786440 | tf_op jit(solution)/shard_map/ppermute | solution.py:24
  13.2 1.3 collective-permute-start.1
  14.5 1.9 %multiply_reduce_fusion.2 = f32[32]{0:T(128)} fusion(f32[32,4,8,128]{3,2,1,0:T(8,128)} %param.8), kind=kLoop, calls=%fused_computation.61 | loop fusion | flops 262112 | bytes 524416 | tf_op jit(solution)/shard_map/reduce_sum | solution.py:71
  19.7 1.5 fusion.73
  23.1 3.5 %collective-permute-start.8 = (s32[8,2,128]{2,1,0:T(2,128)S(1)}, s32[8,2,128]{2,1,0:T(2,128)S(1)}, u32[]{:S(2)}, u32[]{:S(2)}) collective-permute-start(s32[8,2,128]{2,1,0:T(2,128)S(1)} %get-tuple-element.60), channel_id=1, source_target_pairs={{0,4},{4,8},{8,12},{1,5},{5,9},{9,13},{2,6},{6,10},{10,14},{3,7},{... | collective-permute-start | bytes 24584 | tf_op jit(solution)/shard_map/ppermute | solution.py:24
  26.5 1.3 collective-permute-start.9
  28.4 3.6 %collective-permute-done.9 = s32[8,2,128]{2,1,0:T(2,128)S(1)} collective-permute-done((s32[8,2,128]{2,1,0:T(2,128)S(1)}, s32[8,2,128]{2,1,0:T(2,128)S(1)}, u32[]{:S(2)}, u32[]{:S(2)}) %collective-permute-start.9) | collective-permute-done | bytes 8224 | tf_op jit(solution)/shard_map/ppermute | solution.py:27
  32.2 1.3 collective-permute-start.10
  33.5 1.3 collective-permute-start.11
  34.8 1.2 copy.105
  36.0 2.4 %collective-permute-done.11 = s32[8,12,2]{2,1,0:T(8,128)S(1)} collective-permute-done((s32[8,12,2]{2,1,0:T(8,128)S(1)}, s32[8,12,2]{2,1,0:T(8,128)S(1)}, u32[]{:S(2)}, u32[]{:S(2)}) %collective-permute-start.11) | collective-permute-done | bytes 800 | tf_op jit(solution)/shard_map/ppermute | solution.py:27
  38.5 3.9 %select_add_fusion = f32[8,12,132]{2,1,0:T(8,128)S(1)} fusion(f32[]{:T(128)} %bitcast.8, f32[]{:T(128)} %bitcast.7, f32[]{:T(128)} %bitcast.6, f32[]{:T(128)} %bitcast.5, f32[]{:T(128)} %bitcast.4, f32[]{:T(128)} %bitcast.3, s32[8,12,2]{2,1,0:T(8,128)S(1)} %collective-permute-done.11, s32[8,2,128]{2,1,0:T(2,128)S(1)} %collective-permute-done.9, ...), kind=kLoop, calls=%fused_computation.79 | loop fusion | flops 291456 | bytes 101400 | tf_op jit(solution)/shard_map/add | solution.py:35
  43.9 3.5 %collective-permute-start.2 = (f32[32,8,2,128]{3,1,2,0:T(8,128)S(1)}, f32[32,8,2,128]{3,1,2,0:T(8,128)S(1)}, u32[]{:S(2)}, u32[]{:S(2)}) collective-permute-start(f32[32,8,2,128]{3,1,2,0:T(8,128)S(1)} %get-tuple-element.41), channel_id=1, source_target_pairs={{0,4},{4,8},{8,12},{1,5},{5,9},{9,13},{2,6},{6,10},{10,14},{3,7},{... | collective-permute-start | bytes 786440 | tf_op jit(solution)/shard_map/ppermute | solution.py:24
  47.4 1.3 collective-permute-start.3
  49.4 1.7 gather_fusion
  52.1 4.7 %collective-permute-done.3 = f32[32,8,2,128]{3,1,2,0:T(8,128)S(1)} collective-permute-done((f32[32,8,2,128]{3,1,2,0:T(8,128)S(1)}, f32[32,8,2,128]{3,1,2,0:T(8,128)S(1)}, u32[]{:S(2)}, u32[]{:S(2)}) %collective-permute-start.3) | collective-permute-done | bytes 262176 | tf_op jit(solution)/shard_map/ppermute | solution.py:27
  57.9 1.7 fusion.69
  59.7 2.2 %copy.93 = f32[32,8,12,2]{0,1,3,2:T(8,128)S(1)} copy(f32[32,8,12,2]{3,1,2,0:T(8,128)} %get-tuple-element.39) | data formatting | bytes 49152 | tf_op jit(solution)/shard_map/slice | solution.py:25
  61.9 0.9 copy.94
  62.7 1.3 collective-permute-start.5
  64.0 4.2 %collective-permute-start.4 = (f32[32,8,12,2]{0,1,3,2:T(8,128)S(1)}, f32[32,8,12,2]{0,1,3,2:T(8,128)S(1)}, u32[]{:S(2)}, u32[]{:S(2)}) collective-permute-start(f32[32,8,12,2]{0,1,3,2:T(8,128)S(1)} %copy.93), channel_id=1, source_target_pairs={{0,1},{1,2},{2,3},{4,5},{5,6},{6,7},{8,9},{9,10},{10,11},{12,13},{... | collective-permute-start | bytes 73736 | tf_op jit(solution)/shard_map/ppermute | solution.py:24
  74.7 2.4 %copy.95 = f32[32,8,12,2]{3,1,2,0:T(8,128)} copy(f32[32,8,12,2]{0,1,3,2:T(8,128)S(1)} %collective-permute-done.4) | data formatting | bytes 49152 | tf_op jit(solution)/shard_map/ppermute | solution.py:24
  77.1 2.4 %copy.96 = f32[32,8,12,2]{3,1,2,0:T(8,128)} copy(f32[32,8,12,2]{0,1,3,2:T(8,128)S(1)} %collective-permute-done.5) | data formatting | bytes 49152 | tf_op jit(solution)/shard_map/ppermute | solution.py:27
  79.6 4.8 %pad_maximum_fusion = f32[32,8,12,132]{3,1,2,0:T(8,128)S(1)} fusion(f32[32,8,12,2]{3,1,2,0:T(8,128)} %copy.96, f32[32,8,2,128]{3,1,2,0:T(8,128)} %copy-done.11, f32[32,2,8,128]{3,1,2,0:T(2,128)} %copy-done.7, f32[32,4,8,128]{3,1,2,0:T(4,128)} %copy-done.4, f32[32,2,8,128]{3,1,2,0:T(2,128)S(1)} %copy.90, f32[32,8,2,128]{3,1,2,0:T(8,128)} %copy-done.9, ...), kind=kLoop, calls=%fused_computation.8 | loop fusion | flops 2433024 | bytes 3244032 | tf_op jit(solution)/shard_map/concatenate | solution.py:28
  84.5 7.2 %fusion.2 = f32[32,6,10,130]{3,1,2,0:T(8,128)S(1)} fusion(f32[32,8,12,2]{3,1,2,0:T(8,128)S(1)} %copy-done.3, f32[32,8,2,128]{3,1,2,0:T(8,128)S(1)} %copy-done.12, f32[32,8,2,128]{3,1,2,0:T(8,128)S(1)} %copy-done.10, f32[32,2,8,128]{3,1,2,0:T(2,128)S(1)} %copy-done.8, f32[32,4,8,128]{3,1,2,0:T(4,128)S(1)} %copy-done.5, f32[32,2,8,128]{3,1,2,0:T(2,128)S(1)} %copy.90, ...), kind=kLoop, calls=%fused_computation.12 | loop fusion | flops 7238400 | bytes 7799616 | tf_op jit(solution)/shard_map/add | solution.py:59
  91.8 1.5 copy-done.1
  93.3 2.4 %multiply_reduce_fusion.1 = (f32[32]{0:T(128)S(1)}, f32[32]{0:T(128)S(1)}, f32[32]{0:T(128)S(1)}) fusion(f32[32,6,10,130]{3,1,2,0:T(8,128)S(1)} %fusion.2, f32[32,4,8,128]{3,2,1,0:T(8,128)S(1)} %copy-done.6, f32[4,8,128]{2,0,1:T(4,128)S(1)} %copy.111, f32[4,8,128]{2,0,1:T(4,128)S(1)} %copy.110, f32[4,8,128]{2,0,1:T(4,128)S(1)} %copy-done.19, ...), kind=kLoop, calls=%fused_computation.60 | loop fusion | flops 3276704 | bytes 4292992 | tf_op jit(solution)/shard_map/reduce_sum | solution.py:71
  95.7 31.2 %all-reduce = (f32[32]{0:T(128)S(1)}, f32[32]{0:T(128)S(1)}, f32[32]{0:T(128)S(1)}, f32[32]{0:T(128)S(1)}) all-reduce(f32[32]{0:T(128)S(1)} %get-tuple-element.15, f32[32]{0:T(128)S(1)} %get-tuple-element.14, f32[32]{0:T(128)S(1)} %copy-done.32, f32[32]{0:T(128)S(1)} %get-tuple-element.13), channel_id=1, replica_groups=mesh['gx'=2,'gy'=4,'gz'=4] {'gy','gz'}, use_global_device_ids=true, to_apply=%region_10.11 | all-reduce | flops 128 | bytes 1024 | tf_op jit(solution)/shard_map/psum | solution.py:12
  126.9 5.8 %all-reduce.1 = (f32[32]{0:T(128)S(1)}, f32[32]{0:T(128)S(1)}, f32[32]{0:T(128)S(1)}, f32[32]{0:T(128)S(1)}) all-reduce(f32[32]{0:T(128)S(1)} %get-tuple-element.25, f32[32]{0:T(128)S(1)} %get-tuple-element.26, f32[32]{0:T(128)S(1)} %get-tuple-element.27, f32[32]{0:T(128)S(1)} %get-tuple-element.28), channel_id=1, replica_groups=mesh['gx'=2,'gy'=4,'gz'=4] {'gx'}, use_global_device_ids=true, to_apply=%region_11.12 | all-reduce | flops 128 | bytes 1024 | tf_op jit(solution)/shard_map/psum | solution.py:12
  132.7 4.1 %multiply_subtract_fusion = f32[32,6,10,130]{3,1,2,0:T(8,128)} fusion(f32[32,6,10,130]{3,1,2,0:T(8,128)} %copy-done.1, f32[32,8,12,132]{3,1,2,0:T(8,128)S(1)} %pad_maximum_fusion, f32[32]{0:T(128)S(1)} %mul.415, f32[32]{0:T(128)S(1)} %get-tuple-element.35), kind=kLoop, calls=%fused_computation.37 | loop fusion | flops 748800 | bytes 2995456 | tf_op jit(solution)/shard_map/sub | solution.py:109
  136.8 4.8 %copy.122 = f32[32,6,10,130]{0,3,2,1:T(8,128)} copy(f32[32,6,10,130]{3,1,2,0:T(8,128)} %multiply_subtract_fusion) | data formatting | bytes 1996800 | tf_op jit(solution)/shard_map/reshape | solution.py:120
  141.6 4.8 %reshape.172 = f32[32,7800]{0,1:T(8,128)} reshape(f32[32,6,10,130]{0,3,2,1:T(8,128)} %copy.122) | data formatting | bytes 1996800 | tf_op jit(solution)/shard_map/reshape | solution.py:120
  146.4 3.0 %gather_fusion.7 = f32[256,32]{1,0:T(8,128)S(1)} fusion(f32[32,7800]{0,1:T(8,128)} %reshape.172, s32[1024]{0:T(1024)} %get-tuple-element.88), kind=kCustom, calls=%fused_computation.5.clone | custom fusion | bytes 66560 | tf_op jit(solution)/shard_map/jit(_take)/gather | solution.py:125
  149.4 3.0 %gather_fusion.6 = f32[256,32]{1,0:T(8,128)S(1)} fusion(f32[32,7800]{0,1:T(8,128)} %reshape.172, s32[1024]{0:T(1024)} %get-tuple-element.89), kind=kCustom, calls=%fused_computation.4.clone | custom fusion | bytes 66560 | tf_op jit(solution)/shard_map/jit(_take)/gather | solution.py:124
  152.4 3.0 %gather_fusion.5 = f32[256,32]{1,0:T(8,128)S(1)} fusion(f32[32,7800]{0,1:T(8,128)} %reshape.172, s32[1024]{0:T(1024)} %get-tuple-element.90), kind=kCustom, calls=%fused_computation.3.clone | custom fusion | bytes 66560 | tf_op jit(solution)/shard_map/jit(_take)/gather | solution.py:125
  155.4 3.0 %gather_fusion.4 = f32[256,32]{1,0:T(8,128)S(1)} fusion(f32[32,7800]{0,1:T(8,128)} %reshape.172, s32[1024]{0:T(1024)} %get-tuple-element.91), kind=kCustom, calls=%fused_computation.2.clone | custom fusion | bytes 66560 | tf_op jit(solution)/shard_map/jit(_take)/gather | solution.py:124
  158.4 3.0 %gather_fusion.3 = f32[256,32]{1,0:T(8,128)S(1)} fusion(f32[32,7800]{0,1:T(8,128)} %reshape.172, s32[1024]{0:T(1024)} %get-tuple-element.92), kind=kCustom, calls=%fused_computation.1.clone | custom fusion | bytes 66560 | tf_op jit(solution)/shard_map/jit(_take)/gather | solution.py:125
  161.4 3.0 %gather_fusion.2 = f32[256,32]{1,0:T(8,128)S(1)} fusion(f32[32,7800]{0,1:T(8,128)} %reshape.172, s32[1024]{0:T(1024)} %get-tuple-element.93), kind=kCustom, calls=%fused_computation.clone | custom fusion | bytes 66560 | tf_op jit(solution)/shard_map/jit(_take)/gather | solution.py:124
  165.1 1.0 reshape.176
  166.1 3.4 %all-to-all-start = ((f32[8,1,3072]{2,1,0:T(1,128)}), f32[8,1,3072]{2,1,0:T(1,128)S(1)}, u32[]{:S(2)}, u32[]{:S(2)}) async-start(f32[8,1,3072]{2,1,0:T(1,128)} %reshape.176), calls=%async_computation | async-start | bytes 196608 | tf_op jit(solution)/shard_map/all_to_all | solution.py:129
  169.4 7.2 %all-to-all-done = f32[8,1,3072]{2,1,0:T(1,128)S(1)} async-done(((f32[8,1,3072]{2,1,0:T(1,128)}), f32[8,1,3072]{2,1,0:T(1,128)S(1)}, u32[]{:S(2)}, u32[]{:S(2)}) %all-to-all-start) | async-done | bytes 98336 | tf_op jit(solution)/shard_map/all_to_all | solution.py:129
  177.1 0.9 reduce.12
  178.4 0.9 gather_fusion.1
  179.4 1.6 multiply_reduce_fusion.3
  181.4 0.8 copy.121
  (128 shorter events, 19.9 us)
Async XLA Ops:
  0.6 180.4 %copy-start = (f32[32,128]{1,0:T(8,128)S(1)}, f32[32,128]{1,0:T(8,128)}, u32[]{:S(2)}) copy-start(f32[32,128]{1,0:T(8,128)} %param.13) | copy-start | bytes 49156
  1.4 21.7 %collective-permute-start.6 = (s32[2,8,128]{2,1,0:T(8,128)S(1)}, s32[2,8,128]{2,1,0:T(8,128)S(1)}, u32[]{:S(2)}, u32[]{:S(2)}) collective-permute-start(s32[2,8,128]{2,1,0:T(8,128)S(1)} %get-tuple-element.62), channel_id=1, source_target_pairs={{0,16},{1,17},{2,18},{3,19},{4,20},{5,21},{6,22},{7,23},{8,24},{9,... | collective-permute-start | bytes 24584 | tf_op jit(solution)/shard_map/ppermute | solution.py:24
  6.3 16.8 %collective-permute-start.7 = (s32[2,8,128]{2,1,0:T(8,128)S(1)}, s32[2,8,128]{2,1,0:T(8,128)S(1)}, u32[]{:S(2)}, u32[]{:S(2)}) collective-permute-start(s32[2,8,128]{2,1,0:T(8,128)S(1)} %get-tuple-element.63), channel_id=1, source_target_pairs={{16,0},{17,1},{18,2},{19,3},{20,4},{21,5},{22,6},{23,7},{24,8},{25... | collective-permute-start | bytes 24584 | tf_op jit(solution)/shard_map/ppermute | solution.py:27
  8.7 34.8 %collective-permute-start = (f32[32,2,8,128]{3,2,1,0:T(8,128)S(1)}, f32[32,2,8,128]{3,2,1,0:T(8,128)S(1)}, u32[]{:S(2)}, u32[]{:S(2)}) collective-permute-start(f32[32,2,8,128]{3,2,1,0:T(8,128)S(1)} %get-tuple-element.43), channel_id=1, source_target_pairs={{0,16},{1,17},{2,18},{3,19},{4,20},{5,21},{6,22},{7,23},{8,24},{9,... | collective-permute-start | bytes 786440 | tf_op jit(solution)/shard_map/ppermute | solution.py:24
  13.2 30.4 %collective-permute-start.1 = (f32[32,2,8,128]{3,2,1,0:T(8,128)S(1)}, f32[32,2,8,128]{3,2,1,0:T(8,128)S(1)}, u32[]{:S(2)}, u32[]{:S(2)}) collective-permute-start(f32[32,2,8,128]{3,2,1,0:T(8,128)S(1)} %get-tuple-element.44), channel_id=1, source_target_pairs={{16,0},{17,1},{18,2},{19,3},{20,4},{21,5},{22,6},{23,7},{24,8},{25... | collective-permute-start | bytes 786440 | tf_op jit(solution)/shard_map/ppermute | solution.py:27
  23.1 5.4 %collective-permute-start.8 = (s32[8,2,128]{2,1,0:T(2,128)S(1)}, s32[8,2,128]{2,1,0:T(2,128)S(1)}, u32[]{:S(2)}, u32[]{:S(2)}) collective-permute-start(s32[8,2,128]{2,1,0:T(2,128)S(1)} %get-tuple-element.60), channel_id=1, source_target_pairs={{0,4},{4,8},{8,12},{1,5},{5,9},{9,13},{2,6},{6,10},{10,14},{3,7},{... | collective-permute-start | bytes 24584 | tf_op jit(solution)/shard_map/ppermute | solution.py:24
  26.5 5.5 %collective-permute-start.9 = (s32[8,2,128]{2,1,0:T(2,128)S(1)}, s32[8,2,128]{2,1,0:T(2,128)S(1)}, u32[]{:S(2)}, u32[]{:S(2)}) collective-permute-start(s32[8,2,128]{2,1,0:T(2,128)S(1)} %get-tuple-element.61), channel_id=1, source_target_pairs={{4,0},{8,4},{12,8},{5,1},{9,5},{13,9},{6,2},{10,6},{14,10},{7,3},{... | collective-permute-start | bytes 24584 | tf_op jit(solution)/shard_map/ppermute | solution.py:27
  32.2 3.8 %collective-permute-start.10 = (s32[8,12,2]{2,1,0:T(8,128)S(1)}, s32[8,12,2]{2,1,0:T(8,128)S(1)}, u32[]{:S(2)}, u32[]{:S(2)}) collective-permute-start(s32[8,12,2]{2,1,0:T(8,128)S(1)} %get-tuple-element.58), channel_id=1, source_target_pairs={{0,1},{1,2},{2,3},{4,5},{5,6},{6,7},{8,9},{9,10},{10,11},{12,13},{... | collective-permute-start | bytes 2312 | tf_op jit(solution)/shard_map/ppermute | solution.py:24
  33.5 4.9 %collective-permute-start.11 = (s32[8,12,2]{2,1,0:T(8,128)S(1)}, s32[8,12,2]{2,1,0:T(8,128)S(1)}, u32[]{:S(2)}, u32[]{:S(2)}) collective-permute-start(s32[8,12,2]{2,1,0:T(8,128)S(1)} %get-tuple-element.59), channel_id=1, source_target_pairs={{1,0},{2,1},{3,2},{5,4},{6,5},{7,6},{9,8},{10,9},{11,10},{13,12},{... | collective-permute-start | bytes 2312 | tf_op jit(solution)/shard_map/ppermute | solution.py:27
  36.0 20.8 %copy-start.4 = (f32[32,4,8,128]{3,1,2,0:T(4,128)}, f32[32,4,8,128]{3,1,2,0:T(4,128)S(1)}, u32[]{:S(2)}) copy-start(f32[32,4,8,128]{3,1,2,0:T(4,128)S(1)} %copy.105) | copy-start | bytes 1572868
  43.7 14.2 %copy-start.7 = (f32[32,2,8,128]{3,1,2,0:T(2,128)}, f32[32,2,8,128]{3,1,2,0:T(2,128)S(1)}, u32[]{:S(2)}) copy-start(f32[32,2,8,128]{3,1,2,0:T(2,128)S(1)} %copy.92) | copy-start | bytes 786436
  43.9 8.2 %collective-permute-start.2 = (f32[32,8,2,128]{3,1,2,0:T(8,128)S(1)}, f32[32,8,2,128]{3,1,2,0:T(8,128)S(1)}, u32[]{:S(2)}, u32[]{:S(2)}) collective-permute-start(f32[32,8,2,128]{3,1,2,0:T(8,128)S(1)} %get-tuple-element.41), channel_id=1, source_target_pairs={{0,4},{4,8},{8,12},{1,5},{5,9},{9,13},{2,6},{6,10},{10,14},{3,7},{... | collective-permute-start | bytes 786440 | tf_op jit(solution)/shard_map/ppermute | solution.py:24
  47.4 9.4 %collective-permute-start.3 = (f32[32,8,2,128]{3,1,2,0:T(8,128)S(1)}, f32[32,8,2,128]{3,1,2,0:T(8,128)S(1)}, u32[]{:S(2)}, u32[]{:S(2)}) collective-permute-start(f32[32,8,2,128]{3,1,2,0:T(8,128)S(1)} %get-tuple-element.42), channel_id=1, source_target_pairs={{4,0},{8,4},{12,8},{5,1},{9,5},{13,9},{6,2},{10,6},{14,10},{7,3},{... | collective-permute-start | bytes 786440 | tf_op jit(solution)/shard_map/ppermute | solution.py:27
  52.1 4.7 %copy-start.9 = (f32[32,8,2,128]{3,1,2,0:T(8,128)}, f32[32,8,2,128]{3,1,2,0:T(8,128)S(1)}, u32[]{:S(2)}) copy-start(f32[32,8,2,128]{3,1,2,0:T(8,128)S(1)} %collective-permute-done.2) | copy-start | bytes 786436
  56.8 0.7 copy-start.11
  59.6 9.2 %copy-start.25 = (f32[4,8,128]{2,1,0:T(8,128)S(1)}, f32[4,8,128]{2,1,0:T(8,128)}, u32[]{:S(2)}) copy-start(f32[4,8,128]{2,1,0:T(8,128)} %get-tuple-element.50) | copy-start | bytes 49156
  59.6 9.2 %copy-start.24 = (f32[4,8,128]{2,1,0:T(8,128)S(1)}, f32[4,8,128]{2,1,0:T(8,128)}, u32[]{:S(2)}) copy-start(f32[4,8,128]{2,1,0:T(8,128)} %get-tuple-element.45) | copy-start | bytes 49156
  59.6 9.8 %copy-start.23 = (f32[4,8,128]{2,1,0:T(8,128)S(1)}, f32[4,8,128]{2,1,0:T(8,128)}, u32[]{:S(2)}) copy-start(f32[4,8,128]{2,1,0:T(8,128)} %get-tuple-element.46) | copy-start | bytes 49156
  59.7 10.4 %copy-start.22 = (f32[4,8,128]{2,1,0:T(8,128)S(1)}, f32[4,8,128]{2,1,0:T(8,128)}, u32[]{:S(2)}) copy-start(f32[4,8,128]{2,1,0:T(8,128)} %get-tuple-element.47) | copy-start | bytes 49156
  62.7 14.3 %collective-permute-start.5 = (f32[32,8,12,2]{0,1,3,2:T(8,128)S(1)}, f32[32,8,12,2]{0,1,3,2:T(8,128)S(1)}, u32[]{:S(2)}, u32[]{:S(2)}) collective-permute-start(f32[32,8,12,2]{0,1,3,2:T(8,128)S(1)} %copy.94), channel_id=1, source_target_pairs={{1,0},{2,1},{3,2},{5,4},{6,5},{7,6},{9,8},{10,9},{11,10},{13,12},{... | collective-permute-start | bytes 73736 | tf_op jit(solution)/shard_map/ppermute | solution.py:27
  64.0 10.7 %collective-permute-start.4 = (f32[32,8,12,2]{0,1,3,2:T(8,128)S(1)}, f32[32,8,12,2]{0,1,3,2:T(8,128)S(1)}, u32[]{:S(2)}, u32[]{:S(2)}) collective-permute-start(f32[32,8,12,2]{0,1,3,2:T(8,128)S(1)} %copy.93), channel_id=1, source_target_pairs={{0,1},{1,2},{2,3},{4,5},{5,6},{6,7},{8,9},{9,10},{10,11},{12,13},{... | collective-permute-start | bytes 73736 | tf_op jit(solution)/shard_map/ppermute | solution.py:24
  79.5 4.9 %copy-start.2 = (f32[32,8,12,2]{3,1,2,0:T(8,128)S(1)}, f32[32,8,12,2]{3,1,2,0:T(8,128)}, u32[]{:S(2)}) copy-start(f32[32,8,12,2]{3,1,2,0:T(8,128)} %copy.95) | copy-start | bytes 73732
  79.5 4.9 %copy-start.3 = (f32[32,8,12,2]{3,1,2,0:T(8,128)S(1)}, f32[32,8,12,2]{3,1,2,0:T(8,128)}, u32[]{:S(2)}) copy-start(f32[32,8,12,2]{3,1,2,0:T(8,128)} %copy.96) | copy-start | bytes 73732
  79.5 4.9 %copy-start.5 = (f32[32,4,8,128]{3,1,2,0:T(4,128)S(1)}, f32[32,4,8,128]{3,1,2,0:T(4,128)}, u32[]{:S(2)}) copy-start(f32[32,4,8,128]{3,1,2,0:T(4,128)} %copy-done.4) | copy-start | bytes 1572868
  79.5 4.9 %copy-start.8 = (f32[32,2,8,128]{3,1,2,0:T(2,128)S(1)}, f32[32,2,8,128]{3,1,2,0:T(2,128)}, u32[]{:S(2)}) copy-start(f32[32,2,8,128]{3,1,2,0:T(2,128)} %copy-done.7) | copy-start | bytes 786436
  79.5 4.9 %copy-start.10 = (f32[32,8,2,128]{3,1,2,0:T(8,128)S(1)}, f32[32,8,2,128]{3,1,2,0:T(8,128)}, u32[]{:S(2)}) copy-start(f32[32,8,2,128]{3,1,2,0:T(8,128)} %copy-done.9) | copy-start | bytes 786436
  79.5 4.9 %copy-start.12 = (f32[32,8,2,128]{3,1,2,0:T(8,128)S(1)}, f32[32,8,2,128]{3,1,2,0:T(8,128)}, u32[]{:S(2)}) copy-start(f32[32,8,2,128]{3,1,2,0:T(8,128)} %copy-done.11) | copy-start | bytes 786436
  79.5 4.9 %copy-start.13 = (f32[6,10,130]{2,0,1:T(8,128)S(1)}, f32[6,10,130]{2,0,1:T(8,128)}, u32[]{:S(2)}) copy-start(f32[6,10,130]{2,0,1:T(8,128)} %copy.98) | copy-start | bytes 93604
  79.5 4.9 %copy-start.14 = (f32[6,10,130]{2,0,1:T(8,128)S(1)}, f32[6,10,130]{2,0,1:T(8,128)}, u32[]{:S(2)}) copy-start(f32[6,10,130]{2,0,1:T(8,128)} %copy.99) | copy-start | bytes 93604
  79.5 4.9 %copy-start.15 = (f32[6,10,130]{2,0,1:T(8,128)S(1)}, f32[6,10,130]{2,0,1:T(8,128)}, u32[]{:S(2)}) copy-start(f32[6,10,130]{2,0,1:T(8,128)} %copy.97) | copy-start | bytes 93604
  79.5 4.9 %copy-start.16 = (f32[6,10,130]{2,0,1:T(8,128)S(1)}, f32[6,10,130]{2,0,1:T(8,128)}, u32[]{:S(2)}) copy-start(f32[6,10,130]{2,0,1:T(8,128)} %copy.101) | copy-start | bytes 93604
  79.6 4.9 %copy-start.17 = (f32[6,10,130]{2,0,1:T(8,128)S(1)}, f32[6,10,130]{2,0,1:T(8,128)}, u32[]{:S(2)}) copy-start(f32[6,10,130]{2,0,1:T(8,128)} %copy.100) | copy-start | bytes 93604
  84.5 8.8 %copy-start.6 = (f32[32,4,8,128]{3,2,1,0:T(8,128)S(1)}, f32[32,4,8,128]{3,2,1,0:T(8,128)}, u32[]{:S(2)}) copy-start(f32[32,4,8,128]{3,2,1,0:T(8,128)} %param.8) | copy-start | bytes 1572868
  84.5 8.8 %copy-start.18 = (f32[4,8,128]{2,0,1:T(4,128)S(1)}, f32[4,8,128]{2,0,1:T(4,128)}, u32[]{:S(2)}) copy-start(f32[4,8,128]{2,0,1:T(4,128)} %copy.106) | copy-start | bytes 49156
  84.5 8.8 %copy-start.19 = (f32[4,8,128]{2,0,1:T(4,128)S(1)}, f32[4,8,128]{2,0,1:T(4,128)}, u32[]{:S(2)}) copy-start(f32[4,8,128]{2,0,1:T(4,128)} %copy.109) | copy-start | bytes 49156
  84.5 8.8 %copy-start.20 = (f32[4,8,128]{2,0,1:T(4,128)S(1)}, f32[4,8,128]{2,0,1:T(4,128)}, u32[]{:S(2)}) copy-start(f32[4,8,128]{2,0,1:T(4,128)} %copy.108) | copy-start | bytes 49156
  84.5 8.8 %copy-start.21 = (f32[4,8,128]{2,0,1:T(4,128)S(1)}, f32[4,8,128]{2,0,1:T(4,128)}, u32[]{:S(2)}) copy-start(f32[4,8,128]{2,0,1:T(4,128)} %copy.107) | copy-start | bytes 49156
  91.8 1.5 copy-start.1
  93.3 2.4 %copy-start.32 = (f32[32]{0:T(128)S(1)}, f32[32]{0:T(128)}, u32[]{:S(2)}) copy-start(f32[32]{0:T(128)} %multiply_reduce_fusion.2) | copy-start | bytes 388
  141.6 22.8 %copy-start.26 = (f32[256]{0:T(256)S(1)}, f32[256]{0:T(256)}, u32[]{:S(2)}) copy-start(f32[256]{0:T(256)} %select_multiply_fusion) | copy-start | bytes 3076
  141.6 22.8 %copy-start.27 = (pred[256]{0:T(512)(128)(4,1)S(1)}, pred[256]{0:T(512)(128)(4,1)}, u32[]{:S(2)}) copy-start(pred[256]{0:T(512)(128)(4,1)} %get-tuple-element.67) | copy-start | bytes 772
  141.6 22.8 %copy-start.28 = (pred[256]{0:T(512)(128)(4,1)S(1)}, pred[256]{0:T(512)(128)(4,1)}, u32[]{:S(2)}) copy-start(pred[256]{0:T(512)(128)(4,1)} %get-tuple-element.68) | copy-start | bytes 772
  141.6 22.8 %copy-start.29 = (pred[256]{0:T(512)(128)(4,1)S(1)}, pred[256]{0:T(512)(128)(4,1)}, u32[]{:S(2)}) copy-start(pred[256]{0:T(512)(128)(4,1)} %get-tuple-element.69) | copy-start | bytes 772
  141.6 22.8 %copy-start.30 = (pred[256]{0:T(512)(128)(4,1)S(1)}, pred[256]{0:T(512)(128)(4,1)}, u32[]{:S(2)}) copy-start(pred[256]{0:T(512)(128)(4,1)} %get-tuple-element.70) | copy-start | bytes 772
  141.6 22.8 %copy-start.31 = (pred[256]{0:T(512)(128)(4,1)S(1)}, pred[256]{0:T(512)(128)(4,1)}, u32[]{:S(2)}) copy-start(pred[256]{0:T(512)(128)(4,1)} %get-tuple-element.71) | copy-start | bytes 772
  141.6 22.8 %copy-start.33 = (pred[256]{0:T(512)(128)(4,1)S(1)}, pred[256]{0:T(512)(128)(4,1)}, u32[]{:S(2)}) copy-start(pred[256]{0:T(512)(128)(4,1)} %get-tuple-element.33) | copy-start | bytes 772
  149.4 20.0 %copy-start.34 = (s32[128]{0:T(128)S(1)}, s32[128]{0:T(128)}, u32[]{:S(2)}) copy-start(s32[128]{0:T(128)} %param.12) | copy-start | bytes 1540
  166.1 10.6 %all-to-all-start = ((f32[8,1,3072]{2,1,0:T(1,128)}), f32[8,1,3072]{2,1,0:T(1,128)S(1)}, u32[]{:S(2)}, u32[]{:S(2)}) async-start(f32[8,1,3072]{2,1,0:T(1,128)} %reshape.176), calls=%async_computation | async-start | bytes 196608 | tf_op jit(solution)/shard_map/all_to_all | solution.py:129
